TPU v7x, 32 devices: a whole 2x2x4 slice. The times are simulated.
32 devices in a mesh: pipe: 2 (over x), dom: 8 (over z, y), rep: 2 (over core).
Axes of the slice: x: 2, y: 2, z: 4, core: 2. Of those that a mesh axis runs over, the one named last changes fastest.
Arguments:
- handoff: bfloat16 [2, 2, 4096, 512], P('pipe', 'rep', 'dom'), may hold values from -6 to 6
- initial: bfloat16 [2, 2, 4096, 512], P('pipe', 'rep', 'dom'), may hold values from -6 to 6
- cotangent: bfloat16 [2, 2, 4096, 512], P('pipe', 'rep', 'dom'), may hold values from -6 to 6
- slots: int32 [2, 2, 4096, 16], P('pipe', 'rep', 'dom'), may hold values from 0 to 639
- edge_weight: bfloat16 [2, 2, 4096, 16], P('pipe', 'rep', 'dom'), may hold values from 0.029907227 to 0.119628906
- boundary: int32 [2, 2, 8, 2, 64], P('pipe', 'rep', 'dom'), may hold values from 0 to 511
- weights: bfloat16 [4, 512, 512], P('pipe'), may hold values from -0.25 to 0.25
Outputs:
- section_out: bfloat16 [2, 2, 4096, 512], P('pipe', 'rep', 'dom')
- input_grad: bfloat16 [2, 2, 4096, 512], P('pipe', 'rep', 'dom')
- weight_grad: bfloat16 [4, 512, 512], P('pipe')
All inputs are finite; a program needn't handle non-finite values.
Results may differ from a plain program's by a relative error of at most 0.013.
Values may be sent and summed in bfloat16 or wider, within the bound.
A program may use at most 64 MiB of HBM per device.

v0:
```python
import math
import jax
import jax.numpy as jnp
from jax import lax
from jax.sharding import PartitionSpec as P

ALPHA = 0.1


def passed_along(shard, axis, by):
    peers = lax.axis_size(axis)
    return lax.ppermute(shard, axis, [(i, (i + by) % peers) for i in range(peers)])


def adjacency(slot_rows, weight_rows, width):
    columns = jnp.arange(width, dtype=jnp.int32)
    total = jnp.zeros((slot_rows.shape[0], width), jnp.float32)
    for k in range(slot_rows.shape[1]):
        total = total + jnp.where(
            slot_rows[:, k][:, None] == columns[None, :],
            weight_rows[:, k][:, None].astype(jnp.float32),
            jnp.float32(0.0),
        )
    return total.astype(jnp.bfloat16)


def silu_slope(value):
    sig = jax.nn.sigmoid(value)
    return sig * (1.0 + value * (1.0 - sig))


def extend(rows, bound):
    to_prev = rows[bound[0]]
    to_next = rows[bound[1]]
    from_prev = passed_along(to_next, "dom", 1)
    from_next = passed_along(to_prev, "dom", -1)
    return jnp.concatenate([from_prev, rows, from_next], axis=0)


def retract(dext, bound, rows, width):
    own = dext[width : width + rows]
    back_prev = dext[:width]
    back_next = dext[width + rows :]
    from_next = passed_along(back_prev, "dom", -1)
    from_prev = passed_along(back_next, "dom", 1)
    return own.at[bound[0]].add(from_prev).at[bound[1]].add(from_next)


def local(handoff, initial, cotangent, slots, edge_weight, boundary, weights):
    f32 = jnp.float32
    rows = handoff.shape[2]
    width = boundary.shape[-1]
    layers = weights.shape[0]
    scale = 1.0 / math.sqrt(rows * lax.axis_size("dom") * lax.axis_size("rep"))
    segment = lax.axis_index("pipe")
    betas = [
        jnp.log(0.5 / (segment * layers + layer + 1).astype(f32) + 1.0) for layer in range(layers)
    ]
    state = passed_along(handoff[0, 0], "pipe", 1)
    start = initial[0, 0].astype(f32)
    adj = adjacency(slots[0, 0], edge_weight[0, 0], rows + 2 * width)
    bound = boundary[0, 0, 0]
    saved = []
    for layer in range(layers):
        beta = betas[layer]
        ext = extend(state, bound)
        agg = jnp.dot(adj, ext, preferred_element_type=f32)
        s_act = ((1.0 - ALPHA) * agg + ALPHA * start).astype(jnp.bfloat16)
        mixed = jnp.dot(s_act, weights[layer], preferred_element_type=f32)
        z_val = (1.0 - beta) * s_act.astype(f32) + beta * mixed
        state = jax.nn.silu(z_val).astype(jnp.bfloat16)
        saved.append((s_act, z_val))
    grad = passed_along(cotangent[0, 0], "pipe", -1)
    finished = [None] * layers
    for layer in reversed(range(layers)):
        beta = betas[layer]
        s_act, z_val = saved[layer]
        dz_val = (grad.astype(f32) * silu_slope(z_val)).astype(jnp.bfloat16)
        term = lax.dot_general(s_act, dz_val, (((0,), (0,)), ((), ())), preferred_element_type=f32)
        summed = lax.psum(term, ("dom", "rep"))
        finished[layer] = (beta * scale * summed).astype(jnp.bfloat16)
        back = lax.dot_general(
            dz_val, weights[layer], (((1,), (1,)), ((), ())), preferred_element_type=f32
        )
        ds_val = (1.0 - beta) * dz_val.astype(f32) + beta * back
        dagg = ((1.0 - ALPHA) * ds_val).astype(jnp.bfloat16)
        dext = lax.dot_general(adj, dagg, (((0,), (0,)), ((), ())), preferred_element_type=f32)
        grad = retract(dext, bound, rows, width).astype(jnp.bfloat16)
    weight_grad = jnp.stack(finished)
    return (state[None, None], grad[None, None], weight_grad)


def solution(mesh):
    in_specs = (
        P("pipe", "rep", "dom", None),
        P("pipe", "rep", "dom", None),
        P("pipe", "rep", "dom", None),
        P("pipe", "rep", "dom", None),
        P("pipe", "rep", "dom", None),
        P("pipe", "rep", "dom", None, None),
        P("pipe", None, None),
    )
    out_specs = (
        P("pipe", "rep", "dom", None),
        P("pipe", "rep", "dom", None),
        P("pipe", None, None),
    )
    return jax.shard_map(local, mesh=mesh, in_specs=in_specs, out_specs=out_specs, check_vma=False)
```

profile of v0, /device:TPU:0, one launch (start us, length us, event | category | flops | bytes accessed | tf_op | source)
XLA Modules:
  0.0 187.4 jit_solution(13704241570418847226)
XLA Ops:
  7.2 3.0 %collective-permute-start.5 = (bf16[512,512]{1,0:T(8,128)(2,1)}, bf16[512,512]{1,0:T(8,128)(2,1)}, u32[]{:S(2)}, u32[]{:S(2)}) collective-permute-start(bf16[512,512]{1,0:T(8,128)(2,1)} %bitcast.118), channel_id=1, source_target_pairs={{0,16},{16,0},{1,17},{17,1},{2,18},{18,2},{3,19},{19,3},{4,20},{20... | collective-permute-start | bytes 1572872 | tf_op jit(solution)/shard_map/ppermute | solution.py:12
  10.3 0.8 fusion.44
  11.1 1.0 slice_convert_fusion.15
  12.1 1.1 fusion.52
  13.2 20.4 %collective-permute-done = bf16[512,512]{1,0:T(8,128)(2,1)S(1)} collective-permute-done((bf16[512,512]{1,0:T(8,128)(2,1)}, bf16[512,512]{1,0:T(8,128)(2,1)S(1)}, u32[]{:S(2)}, u32[]{:S(2)}) %collective-permute-start) | collective-permute-done | bytes 524320 | tf_op jit(solution)/shard_map/ppermute | solution.py:12
  33.6 0.7 gather_fusion.1
  34.3 4.9 %collective-permute-start.2 = (bf16[64,512]{1,0:T(8,128)(2,1)S(1)}, bf16[64,512]{1,0:T(8,128)(2,1)S(1)}, u32[]{:S(2)}, u32[]{:S(2)}) collective-permute-start(bf16[64,512]{1,0:T(8,128)(2,1)S(1)} %gather_fusion.1), channel_id=1, source_target_pairs={{0,14},{2,0},{4,2},{6,4},{8,6},{10,8},{12,10},{14,12},{1,15},{3,1}... | collective-permute-start | bytes 196616 | tf_op jit(solution)/shard_map/ppermute | solution.py:12
  39.2 0.7 gather_fusion
  39.9 2.9 %add_convert_fusion = bf16[512,640]{1,0:T(8,128)(2,1)S(1)} fusion(f32[512]{0:T(512)S(1)} %bitcast.86, s32[512]{0:T(512)S(1)} %bitcast.102, f32[512]{0:T(512)S(1)} %bitcast.87, s32[512]{0:T(512)S(1)} %bitcast.103, f32[512]{0:T(512)S(1)} %bitcast.88, s32[512]{0:T(512)S(1)} %bitcast.104, f32[512]{0:T(512)S(1)} %bitcast.89, s32[512]{0:T(512)S(1)} %bitcast.105, ...), kind=kLoop, calls=%fused_computation.20 | loop fusion | flops 15728640 | bytes 720896 | tf_op jit(solution)/shard_map/convert_element_type | solution.py:24
  43.0 3.9 %collective-permute-done.1 = bf16[64,512]{1,0:T(8,128)(2,1)S(1)} collective-permute-done((bf16[64,512]{1,0:T(8,128)(2,1)S(1)}, bf16[64,512]{1,0:T(8,128)(2,1)S(1)}, u32[]{:S(2)}, u32[]{:S(2)}) %collective-permute-start.1) | collective-permute-done | bytes 65568 | tf_op jit(solution)/shard_map/ppermute | solution.py:12
  48.3 0.7 gather_fusion.3
  49.0 0.7 gather_fusion.2
  49.7 1.6 collective-permute-start.4
  51.9 2.1 %collective-permute-done.4 = bf16[64,512]{1,0:T(8,128)(2,1)S(1)} collective-permute-done((bf16[64,512]{1,0:T(8,128)(2,1)S(1)}, bf16[64,512]{1,0:T(8,128)(2,1)S(1)}, u32[]{:S(2)}, u32[]{:S(2)}) %collective-permute-start.4) | collective-permute-done | bytes 65568 | tf_op jit(solution)/shard_map/ppermute | solution.py:12
  54.0 4.2 %collective-permute-done.3 = bf16[64,512]{1,0:T(8,128)(2,1)S(1)} collective-permute-done((bf16[64,512]{1,0:T(8,128)(2,1)S(1)}, bf16[64,512]{1,0:T(8,128)(2,1)S(1)}, u32[]{:S(2)}, u32[]{:S(2)}) %collective-permute-start.3) | collective-permute-done | bytes 65568 | tf_op jit(solution)/shard_map/ppermute | solution.py:12
  58.8 3.1 %multiply_convert_fusion.4 = (bf16[512,512]{1,0:T(8,128)(2,1)}, bf16[1,1,512,512]{3,2,1,0:T(8,128)(2,1)}) fusion(bf16[512,512]{1,0:T(8,128)(2,1)} %collective-permute-done.5, bf16[512,512]{1,0:T(8,128)(2,1)S(1)} %fusion.7, bf16[2,512,512]{2,1,0:T(8,128)(2,1)S(1)} %copy-done.7, f32[]{:T(128)S(6)} %log.6, f32[]{:T(128)S(6)} %sub.14), kind=kOutput, calls=%fused_computation.48 | convolution fusion | flops 272629760 | bytes 3145736 | tf_op jit(solution)/shard_map/dot_general | solution.py:69
  61.9 2.2 %fusion.22 = f32[640,512]{1,0:T(8,128)S(1)} fusion(bf16[512,640]{1,0:T(8,128)(2,1)S(1)} %copy-done.1, bf16[512,512]{1,0:T(8,128)(2,1)} %get-tuple-element.9, f32[]{:T(128)S(6)} %log.6, f32[]{:T(128)S(6)} %sub.14, bf16[2,512,512]{2,1,0:T(8,128)(2,1)} %param.13), kind=kOutput, calls=%fused_computation.64 | convolution fusion | flops 605552640 | bytes 3538952 | tf_op jit(solution)/shard_map/dot_general | solution.py:87
  64.8 4.7 %collective-permute-start.7 = (f32[64,512]{1,0:T(8,128)}, f32[64,512]{1,0:T(8,128)S(1)}, u32[]{:S(2)}, u32[]{:S(2)}) collective-permute-start(f32[64,512]{1,0:T(8,128)} %get-tuple-element.7), channel_id=1, source_target_pairs={{0,14},{2,0},{4,2},{6,4},{8,6},{10,8},{12,10},{14,12},{1,15},{3,1}... | collective-permute-start | bytes 393224 | tf_op jit(solution)/shard_map/ppermute | solution.py:12
  69.6 2.6 %fusion.56 = f32[512,512]{1,0:T(8,128)} fusion(bf16[512,512]{1,0:T(8,128)(2,1)} %copy-done.5, bf16[512,512]{1,0:T(8,128)(2,1)} %get-tuple-element.9), kind=kOutput, calls=%fused_computation.113 | convolution fusion | flops 268435456 | bytes 2097152 | tf_op jit(solution)/shard_map/dot_general | solution.py:79
  72.6 1.7 scatter_fusion
  74.4 1.4 scatter_fusion.1
  76.8 1.4 fusion.55
  78.2 1.1 copy-done.2
  79.3 1.9 %fusion.9 = f32[640,512]{1,0:T(8,128)S(1)} fusion(bf16[512,640]{1,0:T(8,128)(2,1)S(1)} %copy-done.2, bf16[512,512]{1,0:T(8,128)(2,1)S(1)} %multiply_convert_fusion.2, f32[]{:T(128)S(6)} %log.7, f32[]{:T(128)S(6)} %sub.15, bf16[2,512,512]{2,1,0:T(8,128)(2,1)} %param.13), kind=kOutput, calls=%fused_computation.40 | convolution fusion | flops 605552640 | bytes 3538952 | tf_op jit(solution)/shard_map/dot_general | solution.py:87
  81.3 4.7 %collective-permute-start.9 = (f32[64,512]{1,0:T(8,128)S(1)}, f32[64,512]{1,0:T(8,128)S(1)}, u32[]{:S(2)}, u32[]{:S(2)}) collective-permute-start(f32[64,512]{1,0:T(8,128)S(1)} %get-tuple-element.5), channel_id=1, source_target_pairs={{0,14},{2,0},{4,2},{6,4},{8,6},{10,8},{12,10},{14,12},{1,15},{3,1}... | collective-permute-start | bytes 393224 | tf_op jit(solution)/shard_map/ppermute | solution.py:12
  86.1 4.0 %collective-permute-done.8 = f32[64,512]{1,0:T(8,128)S(1)} collective-permute-done((f32[64,512]{1,0:T(8,128)S(1)}, f32[64,512]{1,0:T(8,128)S(1)}, u32[]{:S(2)}, u32[]{:S(2)}) %collective-permute-start.8) | collective-permute-done | bytes 131104 | tf_op jit(solution)/shard_map/ppermute | solution.py:12
  90.1 1.4 scatter_fusion.2
  91.5 1.4 scatter_fusion.3
  92.8 0.9 convert_bitcast_fusion
  93.7 83.9 %all-reduce.3.cloned.1.call-done = (f32[512,512]{1,0:T(8,128)}, f32[512,512]{1,0:T(8,128)}) async-done(((f32[512,512]{1,0:T(8,128)}, f32[512,512]{1,0:T(8,128)}), (f32[512,512]{1,0:T(8,128)}, f32[512,512]{1,0:T(8,128)})) %all-reduce.3.cloned.1.call-update) | async-done | bytes 2097168 | tf_op jit(solution)/shard_map/psum | solution.py:80
  177.6 1.8 fusion.23
  179.5 1.1 pad_maximum_fusion
  (39 shorter events, 4.9 us)
Async XLA Ops:
  7.2 39.7 %copy-start.8 = (bf16[1,1,512,512]{3,2,1,0:T(8,128)(2,1)S(1)}, bf16[1,1,512,512]{3,2,1,0:T(8,128)(2,1)}, u32[]{:S(2)}) copy-start(bf16[1,1,512,512]{3,2,1,0:T(8,128)(2,1)} %param.8) | copy-start | bytes 1572868
  7.2 170.5 %all-reduce.3.cloned.1.call-start = ((), (), s32[]{:S(2)}) async-start(), calls=%async_computation | async-start | bytes 4194304 | tf_op jit(solution)/shard_map/psum | solution.py:80
  7.2 51.6 %collective-permute-start.5 = (bf16[512,512]{1,0:T(8,128)(2,1)}, bf16[512,512]{1,0:T(8,128)(2,1)}, u32[]{:S(2)}, u32[]{:S(2)}) collective-permute-start(bf16[512,512]{1,0:T(8,128)(2,1)} %bitcast.118), channel_id=1, source_target_pairs={{0,16},{16,0},{1,17},{17,1},{2,18},{18,2},{3,19},{19,3},{4,20},{20... | collective-permute-start | bytes 1572872 | tf_op jit(solution)/shard_map/ppermute | solution.py:12
  10.3 23.4 %collective-permute-start = (bf16[512,512]{1,0:T(8,128)(2,1)}, bf16[512,512]{1,0:T(8,128)(2,1)S(1)}, u32[]{:S(2)}, u32[]{:S(2)}) collective-permute-start(bf16[512,512]{1,0:T(8,128)(2,1)} %bitcast.117), channel_id=1, source_target_pairs={{0,16},{16,0},{1,17},{17,1},{2,18},{18,2},{3,19},{19,3},{4,20},{20... | collective-permute-start | bytes 1572872 | tf_op jit(solution)/shard_map/ppermute | solution.py:12
  34.3 8.7 %collective-permute-start.2 = (bf16[64,512]{1,0:T(8,128)(2,1)S(1)}, bf16[64,512]{1,0:T(8,128)(2,1)S(1)}, u32[]{:S(2)}, u32[]{:S(2)}) collective-permute-start(bf16[64,512]{1,0:T(8,128)(2,1)S(1)} %gather_fusion.1), channel_id=1, source_target_pairs={{0,14},{2,0},{4,2},{6,4},{8,6},{10,8},{12,10},{14,12},{1,15},{3,1}... | collective-permute-start | bytes 196616 | tf_op jit(solution)/shard_map/ppermute | solution.py:12
  39.9 7.0 %collective-permute-start.1 = (bf16[64,512]{1,0:T(8,128)(2,1)S(1)}, bf16[64,512]{1,0:T(8,128)(2,1)S(1)}, u32[]{:S(2)}, u32[]{:S(2)}) collective-permute-start(bf16[64,512]{1,0:T(8,128)(2,1)S(1)} %gather_fusion), channel_id=1, source_target_pairs={{0,2},{2,4},{4,6},{6,8},{8,10},{10,12},{12,14},{14,0},{1,3},{3,5},... | collective-permute-start | bytes 196616 | tf_op jit(solution)/shard_map/ppermute | solution.py:12
  42.9 15.3 %copy-start = (bf16[512,640]{1,0:T(8,128)(2,1)}, bf16[512,640]{1,0:T(8,128)(2,1)S(1)}, u32[]{:S(2)}) copy-start(bf16[512,640]{1,0:T(8,128)(2,1)S(1)} %add_convert_fusion) | copy-start | bytes 1966084
  43.0 4.5 %copy-start.6 = (bf16[2,512,512]{2,1,0:T(8,128)(2,1)S(1)}, bf16[2,512,512]{2,1,0:T(8,128)(2,1)}, u32[]{:S(2)}) copy-start(bf16[2,512,512]{2,1,0:T(8,128)(2,1)} %param.13) | copy-start | bytes 3145732
  47.5 0.8 copy-start.3
  49.7 4.3 %collective-permute-start.4 = (bf16[64,512]{1,0:T(8,128)(2,1)S(1)}, bf16[64,512]{1,0:T(8,128)(2,1)S(1)}, u32[]{:S(2)}, u32[]{:S(2)}) collective-permute-start(bf16[64,512]{1,0:T(8,128)(2,1)S(1)} %gather_fusion.3), channel_id=1, source_target_pairs={{0,14},{2,0},{4,2},{6,4},{8,6},{10,8},{12,10},{14,12},{1,15},{3,1}... | collective-permute-start | bytes 196616 | tf_op jit(solution)/shard_map/ppermute | solution.py:12
  51.2 7.0 %collective-permute-start.3 = (bf16[64,512]{1,0:T(8,128)(2,1)S(1)}, bf16[64,512]{1,0:T(8,128)(2,1)S(1)}, u32[]{:S(2)}, u32[]{:S(2)}) collective-permute-start(bf16[64,512]{1,0:T(8,128)(2,1)S(1)} %gather_fusion.2), channel_id=1, source_target_pairs={{0,2},{2,4},{4,6},{6,8},{8,10},{10,12},{12,14},{14,0},{1,3},{3,5},... | collective-permute-start | bytes 196616 | tf_op jit(solution)/shard_map/ppermute | solution.py:12
  51.9 7.0 %copy-start.7 = (bf16[2,512,512]{2,1,0:T(8,128)(2,1)S(1)}, bf16[2,512,512]{2,1,0:T(8,128)(2,1)}, u32[]{:S(2)}) copy-start(bf16[2,512,512]{2,1,0:T(8,128)(2,1)} %param.13) | copy-start | bytes 3145732
  58.8 3.1 %copy-start.5 = (bf16[512,512]{1,0:T(8,128)(2,1)}, bf16[512,512]{1,0:T(8,128)(2,1)S(1)}, u32[]{:S(2)}) copy-start(bf16[512,512]{1,0:T(8,128)(2,1)S(1)} %fusion.7) | copy-start | bytes 1572868
  58.8 3.1 %copy-start.1 = (bf16[512,640]{1,0:T(8,128)(2,1)S(1)}, bf16[512,640]{1,0:T(8,128)(2,1)}, u32[]{:S(2)}) copy-start(bf16[512,640]{1,0:T(8,128)(2,1)} %copy-done) | copy-start | bytes 1966084
  64.8 7.8 %collective-permute-start.6 = (f32[64,512]{1,0:T(8,128)S(1)}, f32[64,512]{1,0:T(8,128)}, u32[]{:S(2)}, u32[]{:S(2)}) collective-permute-start(f32[64,512]{1,0:T(8,128)S(1)} %get-tuple-element.8), channel_id=1, source_target_pairs={{0,2},{2,4},{4,6},{6,8},{8,10},{10,12},{12,14},{14,0},{1,3},{3,5},... | collective-permute-start | bytes 393224 | tf_op jit(solution)/shard_map/ppermute | solution.py:12
  64.8 9.5 %collective-permute-start.7 = (f32[64,512]{1,0:T(8,128)}, f32[64,512]{1,0:T(8,128)S(1)}, u32[]{:S(2)}, u32[]{:S(2)}) collective-permute-start(f32[64,512]{1,0:T(8,128)} %get-tuple-element.7), channel_id=1, source_target_pairs={{0,14},{2,0},{4,2},{6,4},{8,6},{10,8},{12,10},{14,12},{1,15},{3,1}... | collective-permute-start | bytes 393224 | tf_op jit(solution)/shard_map/ppermute | solution.py:12
  75.7 1.0 copy-start.4
  78.2 1.1 copy-start.2
  81.2 8.8 %collective-permute-start.8 = (f32[64,512]{1,0:T(8,128)S(1)}, f32[64,512]{1,0:T(8,128)S(1)}, u32[]{:S(2)}, u32[]{:S(2)}) collective-permute-start(f32[64,512]{1,0:T(8,128)S(1)} %get-tuple-element.6), channel_id=1, source_target_pairs={{0,2},{2,4},{4,6},{6,8},{8,10},{10,12},{12,14},{14,0},{1,3},{3,5},... | collective-permute-start | bytes 393224 | tf_op jit(solution)/shard_map/ppermute | solution.py:12
  81.3 10.2 %collective-permute-start.9 = (f32[64,512]{1,0:T(8,128)S(1)}, f32[64,512]{1,0:T(8,128)S(1)}, u32[]{:S(2)}, u32[]{:S(2)}) collective-permute-start(f32[64,512]{1,0:T(8,128)S(1)} %get-tuple-element.5), channel_id=1, source_target_pairs={{0,14},{2,0},{4,2},{6,4},{8,6},{10,8},{12,10},{14,12},{1,15},{3,1}... | collective-permute-start | bytes 393224 | tf_op jit(solution)/shard_map/ppermute | solution.py:12
Sparse Core Ops, SparseCore 0:
  78.3 99.2 all-reduce.2
where the time goes:
time: 188 us; the launch traced here: 187 us
  waiting for transfers between devices  119 us (63%)
  starting transfers between devices  19.6 us (10%)
  other arithmetic  14.7 us (8%)
  between operations  14.5 us (8%)
  matrix products  13.1 us (7%)
  local copies, waits for them, and re-layouts  6.55 us (3%)
    psum x1, waiting for transfers between devices, local(): summed = lax.psum(term, ('dom', 'rep'))  83.9 us
    ppermute x10, waiting for transfers between devices, passed_along(): lax.ppermute(shard, axis, [(i, (i + by) % peers) for i in range(peers)])  35 us
    ppermute x10, starting transfers between devices, passed_along(): lax.ppermute(shard, axis, [(i, (i + by) % peers) for i in range(peers)])  19.6 us
    scatter-add x4, other arithmetic, retract(): return own.at[bound[0]].add(from_prev).at[bound[1]].add(from_next)  5.85 us
    dot_general x2, matrix products, local(): lax.dot_general(adj, dagg, (((0,), (0,)), ((), ())), preferred_element_ty...  4.17 us
    dot_general x2, matrix products, local(): lax.dot_general(s_act, dz_val, (((0,), (0,)), ((), ())), preferred_elemen...  4.05 us
  transfers between devices with their start and end apart: 11, of which 7 were waited for; matrix products, arithmetic and copies ran while one was open for 11% of the time, Pallas kernels for 0%

commit v1 on v0

--- a/solution.py
+++ b/solution.py
@@ -77,7 +77,7 @@
         s_act, z_val = saved[layer]
         dz_val = (grad.astype(f32) * silu_slope(z_val)).astype(jnp.bfloat16)
         term = lax.dot_general(s_act, dz_val, (((0,), (0,)), ((), ())), preferred_element_type=f32)
-        summed = lax.psum(term, ("dom", "rep"))
+        summed = jnp.sum(lax.all_gather(term, ("dom", "rep")), axis=0)
         finished[layer] = (beta * scale * summed).astype(jnp.bfloat16)
         back = lax.dot_general(
             dz_val, weights[layer], (((1,), (1,)), ((), ())), preferred_element_type=f32

time: 188 us -> 333 us (1.77)
  waiting for transfers between devices: 119 us -> 252 us
  other arithmetic: 14.7 us -> 29.1 us
    all_gather x0 -> x2, waiting for transfers between devices: none -> 212 us  [local(): summed = jnp.sum(lax.all_gather(term, ('dom', 'rep')), axis=0)]
    psum x1 -> x0, waiting for transfers between devices: 83.9 us -> none  [local(): summed = lax.psum(term, ('dom', 'rep'))]
    reduce_sum x0 -> x2, other arithmetic: none -> 15.8 us  [local(): summed = jnp.sum(lax.all_gather(term, ('dom', 'rep')), axis=0)]
    ppermute x10, waiting for transfers between devices: 35 us -> 40.3 us  [passed_along(): lax.ppermute(shard, axis, [(i, (i + by) % peers) for i in range(peers)])]
  transfers between devices with their start and end apart: 11 -> 12, of which waited for: 7 -> 9; matrix products, arithmetic and copies ran while one was open for 11% -> 10% of each run, Pallas kernels for 0% -> 0%
where the time goes in v1:
time: 333 us
  waiting for transfers between devices  252 us (76%)
  other arithmetic  29.1 us (9%)
  starting transfers between devices  20.1 us (6%)
  between operations  14.5 us (4%)
  matrix products  11.5 us (3%)
  local copies, waits for them, and re-layouts  5.49 us (2%)
    all_gather x2, waiting for transfers between devices, local(): summed = jnp.sum(lax.all_gather(term, ('dom', 'rep')), axis=0)  212 us
    ppermute x10, waiting for transfers between devices, passed_along(): lax.ppermute(shard, axis, [(i, (i + by) % peers) for i in range(peers)])  40.3 us
    ppermute x10, starting transfers between devices, passed_along(): lax.ppermute(shard, axis, [(i, (i + by) % peers) for i in range(peers)])  20 us
    reduce_sum x2, other arithmetic, local(): summed = jnp.sum(lax.all_gather(term, ('dom', 'rep')), axis=0)  15.8 us
  transfers between devices with their start and end apart: 12, of which 9 were waited for; matrix products, arithmetic and copies ran while one was open for 10% of the time, Pallas kernels for 0%

profile of v1, /device:TPU:0, one launch (start us, length us, event | category | flops | bytes accessed | tf_op | source)
XLA Modules:
  0.0 332.8 jit_solution(1965105019791179191)
XLA Ops:
  7.2 3.0 collective-permute-start.5
  10.3 0.8 fusion.44
  11.1 1.0 slice_convert_fusion.15
  12.1 1.1 fusion.52
  13.2 20.4 %collective-permute-done = bf16[512,512]{1,0:T(8,128)(2,1)S(1)} collective-permute-done((bf16[512,512]{1,0:T(8,128)(2,1)}, bf16[512,512]{1,0:T(8,128)(2,1)S(1)}, u32[]{:S(2)}, u32[]{:S(2)}) %collective-permute-start) | collective-permute-done | bytes 524320 | tf_op jit(solution)/shard_map/ppermute | solution.py:12
  34.3 4.9 %collective-permute-start.2 = (bf16[64,512]{1,0:T(8,128)(2,1)S(1)}, bf16[64,512]{1,0:T(8,128)(2,1)S(1)}, u32[]{:S(2)}, u32[]{:S(2)}) collective-permute-start(bf16[64,512]{1,0:T(8,128)(2,1)S(1)} %gather_fusion.1), channel_id=1, source_target_pairs={{0,14},{2,0},{4,2},{6,4},{8,6},{10,8},{12,10},{14,12},{1,15},{3,1}... | collective-permute-start | bytes 196616 | tf_op jit(solution)/shard_map/ppermute | solution.py:12
  39.9 2.9 add_convert_fusion
  43.0 3.9 %collective-permute-done.1 = bf16[64,512]{1,0:T(8,128)(2,1)S(1)} collective-permute-done((bf16[64,512]{1,0:T(8,128)(2,1)S(1)}, bf16[64,512]{1,0:T(8,128)(2,1)S(1)}, u32[]{:S(2)}, u32[]{:S(2)}) %collective-permute-start.1) | collective-permute-done | bytes 65568 | tf_op jit(solution)/shard_map/ppermute | solution.py:12
  49.0 0.7 gather_fusion.2
  49.7 1.6 collective-permute-start.4
  51.9 2.1 collective-permute-done.4
  54.0 4.2 %collective-permute-done.3 = bf16[64,512]{1,0:T(8,128)(2,1)S(1)} collective-permute-done((bf16[64,512]{1,0:T(8,128)(2,1)S(1)}, bf16[64,512]{1,0:T(8,128)(2,1)S(1)}, u32[]{:S(2)}, u32[]{:S(2)}) %collective-permute-start.3) | collective-permute-done | bytes 65568 | tf_op jit(solution)/shard_map/ppermute | solution.py:12
  58.8 2.7 multiply_convert_fusion.4
  61.5 1.4 fusion.56
  63.0 2.2 fusion.22
  66.0 4.7 %collective-permute-start.7 = (f32[64,512]{1,0:T(8,128)}, f32[64,512]{1,0:T(8,128)S(1)}, u32[]{:S(2)}, u32[]{:S(2)}) collective-permute-start(f32[64,512]{1,0:T(8,128)} %get-tuple-element.5), channel_id=1, source_target_pairs={{0,14},{2,0},{4,2},{6,4},{8,6},{10,8},{12,10},{14,12},{1,15},{3,1}... | collective-permute-start | bytes 393224 | tf_op jit(solution)/shard_map/ppermute | solution.py:12
  70.8 3.1 collective-permute-done.6
  73.8 1.7 scatter_fusion
  75.6 0.8 collective-permute-done.7
  76.4 1.4 scatter_fusion.1
  78.8 1.5 fusion.55
  80.3 1.9 fusion.9
  82.4 5.1 %collective-permute-start.9 = (f32[64,512]{1,0:T(8,128)S(1)}, f32[64,512]{1,0:T(8,128)S(1)}, u32[]{:S(2)}, u32[]{:S(2)}) collective-permute-start(f32[64,512]{1,0:T(8,128)S(1)} %get-tuple-element.3), channel_id=1, source_target_pairs={{0,14},{2,0},{4,2},{6,4},{8,6},{10,8},{12,10},{14,12},{1,15},{3,1}... | collective-permute-start | bytes 393224 | tf_op jit(solution)/shard_map/ppermute | solution.py:12
  87.6 5.7 %collective-permute-done.8 = f32[64,512]{1,0:T(8,128)S(1)} collective-permute-done((f32[64,512]{1,0:T(8,128)S(1)}, f32[64,512]{1,0:T(8,128)S(1)}, u32[]{:S(2)}, u32[]{:S(2)}) %collective-permute-start.8) | collective-permute-done | bytes 131104 | tf_op jit(solution)/shard_map/ppermute | solution.py:12
  93.3 1.4 scatter_fusion.2
  94.7 1.6 scatter_fusion.3
  96.3 0.9 convert_bitcast_fusion
  97.1 93.0 %all-gather.7.cloned.1.call-done = f32[8192,512]{1,0:T(8,128)} async-done(((f32[512,512]{1,0:T(8,128)}), f32[8192,512]{1,0:T(8,128)}) %all-gather.7.cloned.1.call-update) | async-done | bytes 16777232 | tf_op jit(solution)/shard_map/all_gather | solution.py:80
  190.1 7.9 %reduce_sum.19 = f32[512,512]{1,0:T(8,128)S(1)} reduce(f32[16,512,512]{2,1,0:T(8,128)} %bitcast.85, f32[]{:T(128)} %constant.8.clone.1), dimensions={0}, to_apply=%region_5.6 | reduce | flops 3932160 | bytes 17825796 | tf_op jit(solution)/shard_map/reduce_sum | solution.py:80
  198.1 118.7 %all-gather.5.cloned.1.call-done = f32[8192,512]{1,0:T(8,128)} async-done(((f32[512,512]{1,0:T(8,128)}), f32[8192,512]{1,0:T(8,128)}) %all-gather.5.cloned.1.call-update) | async-done | bytes 16777232 | tf_op jit(solution)/shard_map/all_gather | solution.py:80
  316.9 7.9 %reduce_sum.18 = f32[512,512]{1,0:T(8,128)S(1)} reduce(f32[16,512,512]{2,1,0:T(8,128)} %bitcast.86, f32[]{:T(128)} %constant.8.clone.1), dimensions={0}, to_apply=%region_4.5 | reduce | flops 3932160 | bytes 17825796 | tf_op jit(solution)/shard_map/reduce_sum | solution.py:80
  324.9 1.1 pad_maximum_fusion
  (45 shorter events, 7.0 us)
Async XLA Ops:
  7.2 39.7 %copy-start.8 = (bf16[1,1,512,512]{3,2,1,0:T(8,128)(2,1)S(1)}, bf16[1,1,512,512]{3,2,1,0:T(8,128)(2,1)}, u32[]{:S(2)}) copy-start(bf16[1,1,512,512]{3,2,1,0:T(8,128)(2,1)} %param.8) | copy-start | bytes 1572868
  7.2 182.9 %all-gather.7.cloned.1.call-start = ((), (), s32[]{:S(2)}) async-start(), calls=%async_computation.1 | async-start | bytes 17825792 | tf_op jit(solution)/shard_map/all_gather | solution.py:80
  7.2 51.6 %collective-permute-start.5 = (bf16[512,512]{1,0:T(8,128)(2,1)}, bf16[512,512]{1,0:T(8,128)(2,1)}, u32[]{:S(2)}, u32[]{:S(2)}) collective-permute-start(bf16[512,512]{1,0:T(8,128)(2,1)} %bitcast.122), channel_id=1, source_target_pairs={{0,16},{16,0},{1,17},{17,1},{2,18},{18,2},{3,19},{19,3},{4,20},{20... | collective-permute-start | bytes 1572872 | tf_op jit(solution)/shard_map/ppermute | solution.py:12
  10.3 23.4 %collective-permute-start = (bf16[512,512]{1,0:T(8,128)(2,1)}, bf16[512,512]{1,0:T(8,128)(2,1)S(1)}, u32[]{:S(2)}, u32[]{:S(2)}) collective-permute-start(bf16[512,512]{1,0:T(8,128)(2,1)} %bitcast.121), channel_id=1, source_target_pairs={{0,16},{16,0},{1,17},{17,1},{2,18},{18,2},{3,19},{19,3},{4,20},{20... | collective-permute-start | bytes 1572872 | tf_op jit(solution)/shard_map/ppermute | solution.py:12
  34.3 8.7 %collective-permute-start.2 = (bf16[64,512]{1,0:T(8,128)(2,1)S(1)}, bf16[64,512]{1,0:T(8,128)(2,1)S(1)}, u32[]{:S(2)}, u32[]{:S(2)}) collective-permute-start(bf16[64,512]{1,0:T(8,128)(2,1)S(1)} %gather_fusion.1), channel_id=1, source_target_pairs={{0,14},{2,0},{4,2},{6,4},{8,6},{10,8},{12,10},{14,12},{1,15},{3,1}... | collective-permute-start | bytes 196616 | tf_op jit(solution)/shard_map/ppermute | solution.py:12
  39.9 7.0 %collective-permute-start.1 = (bf16[64,512]{1,0:T(8,128)(2,1)S(1)}, bf16[64,512]{1,0:T(8,128)(2,1)S(1)}, u32[]{:S(2)}, u32[]{:S(2)}) collective-permute-start(bf16[64,512]{1,0:T(8,128)(2,1)S(1)} %gather_fusion), channel_id=1, source_target_pairs={{0,2},{2,4},{4,6},{6,8},{8,10},{10,12},{12,14},{14,0},{1,3},{3,5},... | collective-permute-start | bytes 196616 | tf_op jit(solution)/shard_map/ppermute | solution.py:12
  42.9 15.3 %copy-start = (bf16[512,640]{1,0:T(8,128)(2,1)}, bf16[512,640]{1,0:T(8,128)(2,1)S(1)}, u32[]{:S(2)}) copy-start(bf16[512,640]{1,0:T(8,128)(2,1)S(1)} %add_convert_fusion) | copy-start | bytes 1966084
  43.0 4.5 %copy-start.6 = (bf16[2,512,512]{2,1,0:T(8,128)(2,1)S(1)}, bf16[2,512,512]{2,1,0:T(8,128)(2,1)}, u32[]{:S(2)}) copy-start(bf16[2,512,512]{2,1,0:T(8,128)(2,1)} %param.13) | copy-start | bytes 3145732
  47.5 0.8 copy-start.3
  49.7 4.3 %collective-permute-start.4 = (bf16[64,512]{1,0:T(8,128)(2,1)S(1)}, bf16[64,512]{1,0:T(8,128)(2,1)S(1)}, u32[]{:S(2)}, u32[]{:S(2)}) collective-permute-start(bf16[64,512]{1,0:T(8,128)(2,1)S(1)} %gather_fusion.3), channel_id=1, source_target_pairs={{0,14},{2,0},{4,2},{6,4},{8,6},{10,8},{12,10},{14,12},{1,15},{3,1}... | collective-permute-start | bytes 196616 | tf_op jit(solution)/shard_map/ppermute | solution.py:12
  51.3 7.0 %collective-permute-start.3 = (bf16[64,512]{1,0:T(8,128)(2,1)S(1)}, bf16[64,512]{1,0:T(8,128)(2,1)S(1)}, u32[]{:S(2)}, u32[]{:S(2)}) collective-permute-start(bf16[64,512]{1,0:T(8,128)(2,1)S(1)} %gather_fusion.2), channel_id=1, source_target_pairs={{0,2},{2,4},{4,6},{6,8},{8,10},{10,12},{12,14},{14,0},{1,3},{3,5},... | collective-permute-start | bytes 196616 | tf_op jit(solution)/shard_map/ppermute | solution.py:12
  51.9 7.0 %copy-start.7 = (bf16[2,512,512]{2,1,0:T(8,128)(2,1)S(1)}, bf16[2,512,512]{2,1,0:T(8,128)(2,1)}, u32[]{:S(2)}) copy-start(bf16[2,512,512]{2,1,0:T(8,128)(2,1)} %param.13) | copy-start | bytes 3145732
  61.5 1.5 copy-start.5
  61.5 1.5 copy-start.1
  63.0 253.9 %all-gather.5.cloned.1.call-start = ((), (), s32[]{:S(2)}) async-start(), calls=%async_computation | async-start | bytes 17825792 | tf_op jit(solution)/shard_map/all_gather | solution.py:80
  66.0 7.9 %collective-permute-start.6 = (f32[64,512]{1,0:T(8,128)S(1)}, f32[64,512]{1,0:T(8,128)}, u32[]{:S(2)}, u32[]{:S(2)}) collective-permute-start(f32[64,512]{1,0:T(8,128)S(1)} %get-tuple-element.6), channel_id=1, source_target_pairs={{0,2},{2,4},{4,6},{6,8},{8,10},{10,12},{12,14},{14,0},{1,3},{3,5},... | collective-permute-start | bytes 393224 | tf_op jit(solution)/shard_map/ppermute | solution.py:12
  66.0 10.5 %collective-permute-start.7 = (f32[64,512]{1,0:T(8,128)}, f32[64,512]{1,0:T(8,128)S(1)}, u32[]{:S(2)}, u32[]{:S(2)}) collective-permute-start(f32[64,512]{1,0:T(8,128)} %get-tuple-element.5), channel_id=1, source_target_pairs={{0,14},{2,0},{4,2},{6,4},{8,6},{10,8},{12,10},{14,12},{1,15},{3,1}... | collective-permute-start | bytes 393224 | tf_op jit(solution)/shard_map/ppermute | solution.py:12
  77.8 1.0 copy-start.4
  78.8 1.5 copy-start.2
  82.3 11.0 %collective-permute-start.8 = (f32[64,512]{1,0:T(8,128)S(1)}, f32[64,512]{1,0:T(8,128)S(1)}, u32[]{:S(2)}, u32[]{:S(2)}) collective-permute-start(f32[64,512]{1,0:T(8,128)S(1)} %get-tuple-element.4), channel_id=1, source_target_pairs={{0,2},{2,4},{4,6},{6,8},{8,10},{10,12},{12,14},{14,0},{1,3},{3,5},... | collective-permute-start | bytes 393224 | tf_op jit(solution)/shard_map/ppermute | solution.py:12
  82.4 12.3 %collective-permute-start.9 = (f32[64,512]{1,0:T(8,128)S(1)}, f32[64,512]{1,0:T(8,128)S(1)}, u32[]{:S(2)}, u32[]{:S(2)}) collective-permute-start(f32[64,512]{1,0:T(8,128)S(1)} %get-tuple-element.3), channel_id=1, source_target_pairs={{0,14},{2,0},{4,2},{6,4},{8,6},{10,8},{12,10},{14,12},{1,15},{3,1}... | collective-permute-start | bytes 393224 | tf_op jit(solution)/shard_map/ppermute | solution.py:12
Sparse Core Ops, SparseCore 0:
  63.1 126.9 all-gather.6
  192.2 124.5 all-gather.4
